TPU v7x, 128 devices: a whole 4x4x4 slice. The times are simulated.
128 devices in a mesh: row: 8 (over z_lo, y), col: 16 (over z_hi, x, core).
Axes of the slice: x: 4, y: 4, z: 4 (z_hi: 2, z_lo: 2; z = z_hi * 2 + z_lo), core: 2. Of those that a mesh axis runs over, the one named last changes fastest.
Arguments:
- observed: float32 [4, 65536], P(None, ('row', 'col')), may hold values from -50 to 50
- tile_values: bfloat16 [256, 32, 256, 256], P('row', 'col'), may hold values from -2.2649514 to 2.2649514
- tile_cols: int32 [256, 32], P('row', 'col'), may hold values from 0 to 255
Outputs:
- solution: float32 [4, 1048576], P(None, ('col', 'row'))
- residual_ratio: float32 [4], replicated
All inputs are finite; a program needn't handle non-finite values.
Results may differ from a plain program's by a relative error of at most 0.0021.
Values may be sent and summed in bfloat16 or wider, within the bound.
A program may use at most 128 MiB of HBM per device.

v0:
```python
import jax
import jax.numpy as jnp
from jax import lax
from jax.sharding import PartitionSpec as P

ITERS = 2
N = 1048576
epsilon_sq = 1e-06


def local(observed, tile_values, tile_cols):
    right_sides = observed.shape[0]
    row_tiles = tile_values.shape[0]
    per_block = tile_values.shape[1]
    tile_size = tile_values.shape[2]
    col_tiles = N // (tile_size * lax.axis_size("col"))
    panel_len = col_tiles * tile_size
    share_len = panel_len // lax.axis_size("row")
    flat_cols = tile_cols.reshape(-1)

    def adjoint_map(left_bf):
        gathered = lax.all_gather(left_bf, "col", axis=1, tiled=True).reshape(
            right_sides, row_tiles, tile_size
        )
        tile_terms = jnp.einsum(
            "rktj,nrt->nrkj", tile_values, gathered, preferred_element_type=jnp.float32
        )
        tile_terms = tile_terms.reshape(right_sides, row_tiles * per_block, tile_size)
        placed = (
            jnp.zeros((right_sides, col_tiles, tile_size), jnp.float32)
            .at[:, flat_cols]
            .add(tile_terms)
        )
        placed = placed.reshape(right_sides, panel_len)
        summed = lax.psum_scatter(placed, "row", scatter_dimension=1, tiled=True)
        return summed

    def lanczos_pair(left_raw, right_vec):
        beta_sq = lax.psum(jnp.sum(left_raw * left_raw, axis=1), ("row", "col"))
        beta_norm = jnp.sqrt(beta_sq + epsilon_sq)
        product = adjoint_map(left_raw.astype(jnp.bfloat16))
        right_raw = product / beta_norm[:, None] - beta_norm[:, None] * right_vec
        alpha_sq = lax.psum(jnp.sum(right_raw * right_raw, axis=1), ("row", "col"))
        alpha_norm = jnp.sqrt(alpha_sq + epsilon_sq)
        return (beta_norm, alpha_norm, right_raw)

    blank_right = jnp.zeros((right_sides, share_len), jnp.float32)
    beta_norm, alpha_norm, right_raw = lanczos_pair(observed, blank_right)
    first_beta = beta_norm
    left_vec = observed / beta_norm[:, None]
    right_vec = right_raw / alpha_norm[:, None]
    right_bf = right_raw.astype(jnp.bfloat16)
    phibar = beta_norm
    rhobar = alpha_norm
    direction = right_vec
    solution = jnp.zeros_like(right_vec)
    for iteration in range(ITERS):
        whole_panel = lax.all_gather(right_bf, "row", axis=1, tiled=True)
        picked = jnp.take(whole_panel.reshape(right_sides, col_tiles, tile_size), tile_cols, axis=1)
        partial_rows = jnp.einsum(
            "rktj,nrkj->nrt", tile_values, picked, preferred_element_type=jnp.float32
        )
        left_raw = (
            lax.psum_scatter(
                partial_rows.reshape(right_sides, row_tiles * tile_size),
                "col",
                scatter_dimension=1,
                tiled=True,
            )
            / alpha_norm[:, None]
            - alpha_norm[:, None] * left_vec
        )
        beta_norm, alpha_norm, right_raw = lanczos_pair(left_raw, right_vec)
        left_vec = left_raw / beta_norm[:, None]
        right_vec = right_raw / alpha_norm[:, None]
        right_bf = right_raw.astype(jnp.bfloat16)
        rho_val = jnp.sqrt(rhobar * rhobar + beta_norm * beta_norm)
        cosine = rhobar / rho_val
        sine_val = beta_norm / rho_val
        theta_val = sine_val * alpha_norm
        rhobar = -cosine * alpha_norm
        phi_val = cosine * phibar
        phibar = sine_val * phibar
        solution = solution + (phi_val / rho_val)[:, None] * direction
        direction = right_vec - (theta_val / rho_val)[:, None] * direction
    return (solution, phibar / first_beta)


def solution(mesh):
    in_specs = (P(None, ("row", "col")), P("row", "col", None, None), P("row", "col"))
    out_specs = (P(None, ("col", "row")), P())
    return jax.shard_map(local, mesh=mesh, in_specs=in_specs, out_specs=out_specs, check_vma=False)
```

profile of v0, /device:TPU:1, one launch (start us, length us, event | category | flops | bytes accessed | tf_op | source)
XLA Modules:
  0.0 1160.2 jit_solution(9524676217768432283)
XLA Ops:
  8.1 26.5 %all_gather.12 = bf16[4,8192]{1,0:T(4,128)(2,1)S(1)} all-gather(bf16[4,512]{1,0:T(4,128)(2,1)S(1)} %get-tuple-element.13), channel_id=1, replica_groups=mesh['row'=8,'col'=16] {'col'}, dimensions={1}, use_global_device_ids=true | all-gather | bytes 69632 | tf_op jit(solution)/shard_map/all_gather | solution.py:22
  35.5 4.6 fusion.21
  40.2 2.8 scatter_fusion
  43.0 16.1 %copy.26 = f32[4,65536]{0,1:T(8,128)} copy(f32[4,65536]{1,0:T(4,128)S(1)} %bitcast.65) | data formatting | bytes 2097152
  59.2 369.9 %psum.35 = f32[4]{0:T(128)S(1)} all-reduce(f32[4]{0:T(128)S(1)} %get-tuple-element.14), channel_id=1, replica_groups=mesh['row'=8,'col'=16] {'row','col'}, use_global_device_ids=true, to_apply=%region_3.0 | all-reduce | flops 4 | bytes 32 | tf_op jit(solution)/shard_map/psum | solution.py:39
  429.5 2.8 copy.27
  432.6 22.8 %all_gather.13 = bf16[4,65536]{1,0:T(4,128)(2,1)S(1)} all-gather(bf16[4,8192]{1,0:T(4,128)(2,1)S(1)} %convert_element_type.13), channel_id=1, replica_groups=mesh['row'=8,'col'=16] {'row'}, dimensions={1}, use_global_device_ids=true | all-gather | bytes 589824 | tf_op jit(solution)/shard_map/all_gather | solution.py:58
  456.1 5.7 fusion.2
  461.8 2.6 copy.28
  464.5 74.8 %psum.36 = f32[4]{0:T(128)S(1)} all-reduce(f32[4]{0:T(128)S(1)} %get-tuple-element.11), channel_id=1, replica_groups=mesh['row'=8,'col'=16] {'row','col'}, use_global_device_ids=true, to_apply=%region_5.0 | all-reduce | flops 4 | bytes 32 | tf_op jit(solution)/shard_map/psum | solution.py:43
  539.4 8.0 reduce-scatter.15.cloned.1.call-done
  547.4 1.1 copy.29
  548.7 23.2 %all_gather.14 = bf16[4,8192]{1,0:T(4,128)(2,1)S(1)} all-gather(bf16[4,512]{1,0:T(4,128)(2,1)S(1)} %convert_element_type.14), channel_id=1, replica_groups=mesh['row'=8,'col'=16] {'col'}, dimensions={1}, use_global_device_ids=true | all-gather | bytes 69632 | tf_op jit(solution)/shard_map/all_gather | solution.py:22
  571.8 4.6 fusion.22
  576.6 2.8 scatter_fusion.1
  579.4 16.1 %copy.30 = f32[4,65536]{0,1:T(8,128)} copy(f32[4,65536]{1,0:T(4,128)S(1)} %bitcast.64) | data formatting | bytes 2097152
  595.6 371.7 %psum.37 = f32[4]{0:T(128)S(1)} all-reduce(f32[4]{0:T(128)S(1)} %get-tuple-element.9), channel_id=1, replica_groups=mesh['row'=8,'col'=16] {'row','col'}, use_global_device_ids=true, to_apply=%region_8.10 | all-reduce | flops 4 | bytes 32 | tf_op jit(solution)/shard_map/psum | solution.py:39
  967.3 2.8 copy.31
  970.3 23.0 %all_gather.15 = bf16[4,65536]{1,0:T(4,128)(2,1)S(1)} all-gather(bf16[4,8192]{1,0:T(4,128)(2,1)S(1)} %get-tuple-element.7), channel_id=1, replica_groups=mesh['row'=8,'col'=16] {'row'}, dimensions={1}, use_global_device_ids=true | all-gather | bytes 589824 | tf_op jit(solution)/shard_map/all_gather | solution.py:58
  994.0 5.7 fusion
  999.7 2.6 copy.32
  1002.5 75.0 %psum.38 = f32[4]{0:T(128)S(1)} all-reduce(f32[4]{0:T(128)S(1)} %multiply_reduce_fusion), channel_id=1, replica_groups=mesh['row'=8,'col'=16] {'row','col'}, use_global_device_ids=true, to_apply=%region_12.14 | all-reduce | flops 4 | bytes 32 | tf_op jit(solution)/shard_map/psum | solution.py:43
  1077.5 8.0 reduce-scatter.19.cloned.1.call-done
  1086.7 65.6 %psum.39 = f32[4]{0:T(128)S(1)} all-reduce(f32[4]{0:T(128)S(1)} %fusion.11), channel_id=1, replica_groups=mesh['row'=8,'col'=16] {'row','col'}, use_global_device_ids=true, to_apply=%region_15.17 | all-reduce | flops 4 | bytes 32 | tf_op jit(solution)/shard_map/psum | solution.py:39
  (43 shorter events, 7.5 us)
Async XLA Ops:
  7.2 422.3 %reduce-scatter.13.cloned.1.call-start = ((), (), s32[]{:S(2)}) async-start(), calls=%async_computation.4 | async-start | bytes 37748736
  59.1 370.0 %copy-start.1 = (s32[32,2]{0,1:T(2,128)S(1)}, s32[32,2]{0,1:T(2,128)}, u32[]{:S(2)}) copy-start(s32[32,2]{0,1:T(2,128)} %param.7) | copy-start | bytes 772
  59.1 488.2 %reduce-scatter.15.cloned.1.call-start = ((), (), s32[]{:S(2)}) async-start(), calls=%async_computation.5 | async-start | bytes 4456448
  456.1 92.3 %copy-start = (f32[4,512]{1,0:T(4,128)S(1)}, f32[4,512]{1,0:T(4,128)}, u32[]{:S(2)}) copy-start(f32[4,512]{1,0:T(4,128)} %param.5) | copy-start | bytes 24580
  464.5 502.9 %reduce-scatter.17.cloned.1.call-start = ((), (), s32[]{:S(2)}) async-start(), calls=%async_computation.6 | async-start | bytes 37748736
  595.5 490.0 %reduce-scatter.19.cloned.1.call-start = ((), (), s32[]{:S(2)}) async-start(), calls=%async_computation.7 | async-start | bytes 4456448
Sparse Core Ops, SparseCore 0:
  59.3 325.6 reduce-scatter.12
  464.6 82.7 reduce-scatter.14
  595.6 327.5 reduce-scatter.16
  1002.6 82.7 reduce-scatter.18
where the time goes:
time: 1160 us
  blocking collectives  1050 us (91%)
  local copies, waits for them, and re-layouts  48 us (4%)
  matrix products  20.5 us (2%)
  waiting for transfers between devices  16.1 us (1%)
  between operations  13.9 us (1%)
    psum x3, blocking collectives, lanczos_pair(): beta_sq = lax.psum(jnp.sum(left_raw * left_raw, axis=1), ('row', 'col'))  807 us
    psum x2, blocking collectives, lanczos_pair(): alpha_sq = lax.psum(jnp.sum(right_raw * right_raw, axis=1), ('row', 'col'))  150 us
    all_gather x2, blocking collectives, adjoint_map(): lax.all_gather(left_bf, 'col', axis=1, tiled=True)  49.7 us
    unnamed x13, local copies, waits for them, and re-layouts  46 us
    all_gather x2, blocking collectives, local(): whole_panel = lax.all_gather(right_bf, 'row', axis=1, tiled=True)  45.8 us
  transfers between devices with their start and end apart: 4, of which 2 were waited for; matrix products, arithmetic and copies ran while one was open for 0% of the time, Pallas kernels for 0%

commit v1 on v0

--- a/solution.py
+++ b/solution.py
@@ -6,6 +6,13 @@
 ITERS = 2
 N = 1048576
 epsilon_sq = 1e-06
+
+
+def all_by_exchange(shard, axis, d):
+    size = lax.axis_size(axis)
+    shards = jnp.stack([shard for _ in range(size)])
+    shards = lax.all_to_all(shards, axis, split_axis=0, concat_axis=0)
+    return jnp.concatenate(shards, axis=d)
 
 
 def local(observed, tile_values, tile_cols):
@@ -55,7 +62,7 @@
     direction = right_vec
     solution = jnp.zeros_like(right_vec)
     for iteration in range(ITERS):
-        whole_panel = lax.all_gather(right_bf, "row", axis=1, tiled=True)
+        whole_panel = all_by_exchange(right_bf, "row", 1)
         picked = jnp.take(whole_panel.reshape(right_sides, col_tiles, tile_size), tile_cols, axis=1)
         partial_rows = jnp.einsum(
             "rktj,nrkj->nrt", tile_values, picked, preferred_element_type=jnp.float32

time: 1160 us -> 1240 us (1.069)
  waiting for transfers between devices: 16.1 us -> 151 us
  blocking collectives: 1050 us -> 988 us
    unnamed x8, waiting for transfers between devices: 16.1 us -> 151 us
    all_gather x2 -> x0, blocking collectives: 45.8 us -> none  [local(): whole_panel = lax.all_gather(right_bf, 'row', axis=1, tiled=True)]
    psum x2, blocking collectives: 150 us -> 131 us  [lanczos_pair(): alpha_sq = lax.psum(jnp.sum(right_raw * right_raw, axis=1), ('row', 'col'))]
  transfers between devices with their start and end apart: 4 -> 6, of which waited for: 2 -> 2; matrix products, arithmetic and copies ran while one was open for 0% -> 0% of each run, Pallas kernels for 0% -> 0%
where the time goes in v1:
time: 1240 us
  blocking collectives  988 us (80%)
  waiting for transfers between devices  151 us (12%)
  local copies, waits for them, and re-layouts  49.9 us (4%)
  matrix products  20.5 us (2%)
  between operations  13.9 us (1%)
    psum x3, blocking collectives, lanczos_pair(): beta_sq = lax.psum(jnp.sum(left_raw * left_raw, axis=1), ('row', 'col'))  808 us
    unnamed x8, waiting for transfers between devices  151 us
    psum x2, blocking collectives, lanczos_pair(): alpha_sq = lax.psum(jnp.sum(right_raw * right_raw, axis=1), ('row', 'col'))  131 us
    all_gather x2, blocking collectives, adjoint_map(): lax.all_gather(left_bf, 'col', axis=1, tiled=True)  49.6 us
    unnamed x13, local copies, waits for them, and re-layouts  46 us
  transfers between devices with their start and end apart: 6, of which 2 were waited for; matrix products, arithmetic and copies ran while one was open for 0% of the time, Pallas kernels for 0%

profile of v1, /device:TPU:1, one launch (start us, length us, event | category | flops | bytes accessed | tf_op | source)
XLA Modules:
  0.0 1240.2 jit_solution(4951896587201468946)
XLA Ops:
  8.1 26.5 %all_gather.6 = bf16[4,8192]{1,0:T(4,128)(2,1)S(1)} all-gather(bf16[4,512]{1,0:T(4,128)(2,1)S(1)} %get-tuple-element.13), channel_id=1, replica_groups=mesh['row'=8,'col'=16] {'col'}, dimensions={1}, use_global_device_ids=true | all-gather | bytes 69632 | tf_op jit(solution)/shard_map/all_gather | solution.py:29
  35.5 4.6 fusion.21
  40.2 2.8 scatter_fusion
  43.0 16.1 %copy.30 = f32[4,65536]{0,1:T(8,128)} copy(f32[4,65536]{1,0:T(4,128)S(1)} %bitcast.69) | data formatting | bytes 2097152
  59.1 370.0 %psum.35 = f32[4]{0:T(128)S(1)} all-reduce(f32[4]{0:T(128)S(1)} %get-tuple-element.14), channel_id=1, replica_groups=mesh['row'=8,'col'=16] {'row','col'}, use_global_device_ids=true, to_apply=%region_3.0 | all-reduce | flops 4 | bytes 32 | tf_op jit(solution)/shard_map/psum | solution.py:46
  429.1 2.8 copy.31
  433.2 3.5 all-to-all-start
  437.1 65.5 %psum.36 = f32[4]{0:T(128)S(1)} all-reduce(f32[4]{0:T(128)S(1)} %get-tuple-element.11), channel_id=1, replica_groups=mesh['row'=8,'col'=16] {'row','col'}, use_global_device_ids=true, to_apply=%region_5.0 | all-reduce | flops 4 | bytes 32 | tf_op jit(solution)/shard_map/psum | solution.py:50
  503.3 5.7 fusion.2
  508.9 2.6 copy.32
  511.7 75.6 %reduce-scatter.15.cloned.1.call-done = f32[512,4]{1,0:T(8,128)} async-done(((f32[8192,4]{1,0:T(8,128)}), f32[512,4]{1,0:T(8,128)}) %reduce-scatter.15.cloned.1.call-update) | async-done | bytes 8208
  587.3 1.1 copy.33
  588.6 23.2 %all_gather.7 = bf16[4,8192]{1,0:T(4,128)(2,1)S(1)} all-gather(bf16[4,512]{1,0:T(4,128)(2,1)S(1)} %convert_element_type.14), channel_id=1, replica_groups=mesh['row'=8,'col'=16] {'col'}, dimensions={1}, use_global_device_ids=true | all-gather | bytes 69632 | tf_op jit(solution)/shard_map/all_gather | solution.py:29
  611.7 4.6 fusion.22
  616.4 2.8 scatter_fusion.1
  619.3 16.1 %copy.34 = f32[4,65536]{0,1:T(8,128)} copy(f32[4,65536]{1,0:T(4,128)S(1)} %bitcast.68) | data formatting | bytes 2097152
  635.4 372.0 %psum.37 = f32[4]{0:T(128)S(1)} all-reduce(f32[4]{0:T(128)S(1)} %get-tuple-element.9), channel_id=1, replica_groups=mesh['row'=8,'col'=16] {'row','col'}, use_global_device_ids=true, to_apply=%region_8.10 | all-reduce | flops 4 | bytes 32 | tf_op jit(solution)/shard_map/psum | solution.py:46
  1007.4 2.8 copy.35
  1011.4 3.5 all-to-all-start.1
  1015.1 65.5 %psum.38 = f32[4]{0:T(128)S(1)} all-reduce(f32[4]{0:T(128)S(1)} %multiply_reduce_fusion), channel_id=1, replica_groups=mesh['row'=8,'col'=16] {'row','col'}, use_global_device_ids=true, to_apply=%region_12.14 | all-reduce | flops 4 | bytes 32 | tf_op jit(solution)/shard_map/psum | solution.py:50
  1081.3 5.7 fusion
  1086.9 2.6 copy.36
  1089.6 75.7 %reduce-scatter.19.cloned.1.call-done = f32[512,4]{1,0:T(8,128)} async-done(((f32[8192,4]{1,0:T(8,128)}), f32[512,4]{1,0:T(8,128)}) %reduce-scatter.19.cloned.1.call-update) | async-done | bytes 8208
  1166.5 65.8 %psum.39 = f32[4]{0:T(128)S(1)} all-reduce(f32[4]{0:T(128)S(1)} %fusion.11), channel_id=1, replica_groups=mesh['row'=8,'col'=16] {'row','col'}, use_global_device_ids=true, to_apply=%region_15.17 | all-reduce | flops 4 | bytes 32 | tf_op jit(solution)/shard_map/psum | solution.py:46
  (47 shorter events, 9.3 us)
Async XLA Ops:
  7.2 421.9 %reduce-scatter.13.cloned.1.call-start = ((), (), s32[]{:S(2)}) async-start(), calls=%async_computation.6 | async-start | bytes 37748736
  59.1 377.6 %copy-start.1 = (s32[32,2]{0,1:T(2,128)S(1)}, s32[32,2]{0,1:T(2,128)}, u32[]{:S(2)}) copy-start(s32[32,2]{0,1:T(2,128)} %param.7) | copy-start | bytes 772
  433.2 69.4 %all-to-all-start = ((bf16[8,4,8192]{2,1,0:T(4,128)(2,1)}), bf16[8,4,8192]{2,1,0:T(4,128)(2,1)S(1)}, u32[]{:S(2)}, u32[]{:S(2)}) async-start(bf16[8,4,8192]{2,1,0:T(4,128)(2,1)} %stack.4), calls=%async_computation | async-start | bytes 1048576 | tf_op jit(solution)/shard_map/all_to_all | solution.py:14
  436.7 150.6 %reduce-scatter.15.cloned.1.call-start = ((), (), s32[]{:S(2)}) async-start(), calls=%async_computation.7 | async-start | bytes 4456448
  503.3 85.1 %copy-start = (f32[4,512]{1,0:T(4,128)S(1)}, f32[4,512]{1,0:T(4,128)}, u32[]{:S(2)}) copy-start(f32[4,512]{1,0:T(4,128)} %param.5) | copy-start | bytes 24580
  511.6 495.8 %reduce-scatter.17.cloned.1.call-start = ((), (), s32[]{:S(2)}) async-start(), calls=%async_computation.8 | async-start | bytes 37748736
  1011.4 69.2 %all-to-all-start.1 = ((bf16[8,4,8192]{2,1,0:T(4,128)(2,1)}), bf16[8,4,8192]{2,1,0:T(4,128)(2,1)S(1)}, u32[]{:S(2)}, u32[]{:S(2)}) async-start(bf16[8,4,8192]{2,1,0:T(4,128)(2,1)} %stack.5), calls=%async_computation.1 | async-start | bytes 1048576 | tf_op jit(solution)/shard_map/all_to_all | solution.py:14
  1014.9 150.4 %reduce-scatter.19.cloned.1.call-start = ((), (), s32[]{:S(2)}) async-start(), calls=%async_computation.9 | async-start | bytes 4456448
Sparse Core Ops, SparseCore 0:
  59.3 325.7 reduce-scatter.12
  511.7 75.5 reduce-scatter.14
  635.5 327.8 reduce-scatter.16
  1089.7 75.5 reduce-scatter.18
